TPU v7x, 256 devices: a whole 4x4x8 slice. The times are simulated.
256 devices in a mesh: seq: 64 (over x_hi, z, y), tp: 4 (over x_lo, core).
Axes of the slice: x: 4 (x_hi: 2, x_lo: 2; x = x_hi * 2 + x_lo), y: 4, z: 8, core: 2. Of those that a mesh axis runs over, the one named last changes fastest.
Arguments:
- query_rows: bfloat16 [16384, 4096], P('seq', 'tp'), may hold values from -130 to 130
- key_rows: bfloat16 [16384, 4096], P('seq', 'tp'), may hold values from -8 to 8
- value_rows: bfloat16 [16384, 4096], P('seq', 'tp'), may hold values from -6 to 6
- cotangent: bfloat16 [16384, 4096], P('seq', 'tp'), may hold values from -6 to 6
- global_pos: int32 [256], P('seq'), may hold values from 0 to 16383, as said below
- partner_mask: int32 [1], replicated, may hold values from 1 to 63
- rand_block: int32 [1, 64], replicated, may hold values from 0 to 1
Outputs:
- attention: bfloat16 [16384, 4096], P('seq', 'tp')
- grad_queries: bfloat16 [16384, 4096], P('seq', 'tp')
- grad_keys: bfloat16 [16384, 4096], P('seq', 'tp')
- grad_values: bfloat16 [16384, 4096], P('seq', 'tp')
Inputs may be any that keep to these rules, and one draw needn't show every extreme that they name: `global_pos`: the tokens of run d (positions d * 256 onward) hold exactly 4 global positions; all are distinct and in increasing order.
All inputs are finite; a program needn't handle non-finite values.
Results may differ from a plain program's by a relative error of at most 0.011.
Values may be sent and summed in bfloat16 or wider, within the bound.
A program may use at most 128 MiB of HBM per device.

v0:
```python
import jax
import jax.numpy as jnp
from jax import lax
from jax.sharding import PartitionSpec as P

HEAD_DIM = 128
BLK = 128


def from_partner(shard, axis, bit):
    return lax.ppermute(shard, axis, [(i, i ^ 1 << bit) for i in range(lax.axis_size(axis))])


def with_halo(shard, sides, width):
    for axis, dim in sides:
        size, length = (lax.axis_size(axis), shard.shape[dim])
        up = [(i, (i + 1) % size) for i in range(size - 1)]
        down = [(j, i) for i, j in up]
        last = lax.slice_in_dim(shard, length - width, length, axis=dim)
        first = lax.slice_in_dim(shard, 0, width, axis=dim)
        before = lax.ppermute(last, axis, up)
        after = lax.ppermute(first, axis, down)
        shard = jnp.concatenate([before, shard, after], axis=dim)
    return shard


def joined(value, axis, join):
    pieces = jax.tree.map(lambda part: lax.all_gather(part, axis), value)
    head = jax.tree.map(lambda part: part[0], pieces)
    tail = jax.tree.map(lambda part: part[1:], pieces)
    total, _ = lax.scan(lambda total, piece: (join(total, piece), None), head, tail)
    return total


def passed_along(block, axis, distance):
    devices = range(lax.axis_size(axis))
    route = [(i - distance, i) for i in devices if i - distance in devices]
    return lax.ppermute(block, axis, route)


def attend(query_inputs, gathered_keys, gathered_values, usable, incoming_gradient):
    softmax_scale_factor = query_inputs.shape[-1] ** (-0.5)
    logit_scores = (
        jnp.einsum("crj,prj->rcp", query_inputs, gathered_keys, preferred_element_type=jnp.float32)
        * softmax_scale_factor
    )
    logit_scores = jnp.where(usable[None, None, :], logit_scores, -1e30)
    maxima = jnp.max(logit_scores, axis=2, keepdims=True)
    raised = jnp.exp(logit_scores - maxima)
    totals = jnp.sum(raised, axis=2, keepdims=True)
    chances = raised / totals
    attention_weight_rows = chances.astype(jnp.bfloat16)
    attention_output = jnp.einsum(
        "bxl,lby->xby", attention_weight_rows, gathered_values, preferred_element_type=jnp.float32
    ).astype(jnp.bfloat16)
    deltas = jnp.transpose(
        jnp.sum(
            incoming_gradient.astype(jnp.float32) * attention_output.astype(jnp.float32), axis=2
        )
    )[:, :, None]
    probability_gradient = jnp.einsum(
        "crj,prj->rcp", incoming_gradient, gathered_values, preferred_element_type=jnp.float32
    )
    scaled_scores = (chances * (probability_gradient - deltas) * softmax_scale_factor).astype(
        jnp.bfloat16
    )
    query_gradient_rows = jnp.einsum(
        "bxl,lby->xby", scaled_scores, gathered_keys, preferred_element_type=jnp.float32
    )
    key_gradient_rows = jnp.einsum(
        "cgi,gcx->icx", scaled_scores, query_inputs, preferred_element_type=jnp.float32
    )
    value_gradient_rows = jnp.einsum(
        "cgi,gcx->icx", attention_weight_rows, incoming_gradient, preferred_element_type=jnp.float32
    )
    return (attention_output, query_gradient_rows, key_gradient_rows, value_gradient_rows)


def merge_stats(first, second):
    maxima = jnp.maximum(first[0], second[0])
    totals = first[1] * jnp.exp(first[0] - maxima) + second[1] * jnp.exp(second[0] - maxima)
    return (maxima, totals)


def level_order(levels):
    return list(range(levels))


def send_blocks(parcel, partner_mask, levels):
    for bit_level in level_order(levels):
        swapped = from_partner(parcel, "seq", bit_level)
        selected = jnp.right_shift(partner_mask, bit_level) % 2 == 1
        parcel = jnp.where(selected[:, None, None], swapped, parcel)
    return parcel


def return_grads(parcel, partner_mask, levels):
    for bit_level in level_order(levels):
        swapped = from_partner(parcel.astype(jnp.bfloat16), "seq", bit_level).astype(parcel.dtype)
        selected = jnp.right_shift(partner_mask, bit_level) % 2 == 1
        parcel = jnp.where(selected[:, None, None], swapped, parcel)
    return parcel


def per_device(query_rows, key_rows, value_rows, cotangent, global_pos, partner_mask, rand_block):
    local_count, columns = query_rows.shape
    head_here = columns // HEAD_DIM
    block_here = local_count // BLK
    rounds_count = partner_mask.shape[0]
    global_here = global_pos.shape[0]
    shard_index = lax.axis_index("seq")
    shard_count = lax.axis_size("seq")
    levels = shard_count.bit_length() - 1
    local_pos = global_pos - shard_index * local_count
    global_query, global_key, global_value, global_cot = (
        lax.all_gather(query_rows[local_pos], "seq", axis=0, tiled=True),
        lax.all_gather(key_rows[local_pos], "seq", axis=0, tiled=True),
        lax.all_gather(value_rows[local_pos], "seq", axis=0, tiled=True),
        lax.all_gather(cotangent[local_pos], "seq", axis=0, tiled=True),
    )
    global_count = global_query.shape[0]
    key_value = jnp.concatenate([key_rows, value_rows], axis=1)
    extended = with_halo(key_value, (("seq", 0),), BLK)
    requester = jnp.bitwise_xor(shard_index, partner_mask)
    chosen = rand_block[jnp.arange(rounds_count, dtype=jnp.int32), requester]
    outgoing = jnp.stack([lax.dynamic_slice_in_dim(key_value, chosen[0] * BLK, BLK, 0)])
    incoming = send_blocks(outgoing, partner_mask, levels)
    random_rows = incoming.reshape(rounds_count * BLK, 2 * columns)
    shared_keys = jnp.concatenate([random_rows[:, :columns], global_key], axis=0)
    shared_values = jnp.concatenate([random_rows[:, columns:], global_value], axis=0)
    shared_count = shared_keys.shape[0]
    global_marks = jnp.any(
        jnp.arange(local_count, dtype=jnp.int32)[:, None] == local_pos[None, :], axis=1
    )
    sparse_cot = jnp.where(global_marks[:, None], jnp.zeros_like(cotangent), cotangent)
    first_block = shard_index * block_here
    last_block = shard_count * block_here - 1

    def block_step(carried, number):
        begin = number * BLK
        window = lax.dynamic_slice_in_dim(extended, begin, 3 * BLK, 0)
        gathered_keys = jnp.concatenate([window[:, :columns], shared_keys], axis=0).reshape(
            -1, head_here, HEAD_DIM
        )
        gathered_values = jnp.concatenate([window[:, columns:], shared_values], axis=0).reshape(
            -1, head_here, HEAD_DIM
        )
        global_block = first_block + number
        usable = jnp.concatenate(
            [
                jnp.full((BLK,), global_block > 0),
                jnp.ones((BLK,), bool),
                jnp.full((BLK,), global_block < last_block),
                jnp.ones((shared_count,), bool),
            ]
        )
        attention_output, query_gradient_rows, key_gradient_rows, value_gradient_rows = attend(
            lax.dynamic_slice_in_dim(query_rows, begin, BLK, 0).reshape(BLK, head_here, HEAD_DIM),
            gathered_keys,
            gathered_values,
            usable,
            lax.dynamic_slice_in_dim(sparse_cot, begin, BLK, 0).reshape(BLK, head_here, HEAD_DIM),
        )
        key_flat = key_gradient_rows.reshape(-1, columns)
        value_flat = value_gradient_rows.reshape(-1, columns)
        return (
            carried,
            (
                attention_output.reshape(BLK, columns),
                query_gradient_rows.reshape(BLK, columns),
                key_flat[: 3 * BLK],
                value_flat[: 3 * BLK],
                key_flat[3 * BLK :],
                value_flat[3 * BLK :],
            ),
        )

    unused = jnp.zeros((), jnp.float32)
    unused, (sparse_out, sparse_dq, window_dk, window_dv, shared_dk, shared_dv) = lax.scan(
        block_step, unused, jnp.arange(block_here, dtype=jnp.int32)
    )
    sparse_out = sparse_out.reshape(local_count, columns)
    sparse_dq = sparse_dq.reshape(local_count, columns)
    ext_keys = jnp.zeros((local_count + 2 * BLK, columns), jnp.float32)
    ext_values = jnp.zeros((local_count + 2 * BLK, columns), jnp.float32)
    for block_number in range(block_here):
        lower = block_number * BLK
        ext_keys = ext_keys.at[lower : lower + 3 * BLK].add(window_dk[block_number])
        ext_values = ext_values.at[lower : lower + 3 * BLK].add(window_dv[block_number])
    grad_ext = jnp.concatenate([ext_keys, ext_values], axis=1)
    grad_shared = jnp.concatenate([jnp.sum(shared_dk, axis=0), jnp.sum(shared_dv, axis=0)], axis=1)
    softmax_scale_factor = HEAD_DIM ** (-0.5)
    query_per_head = global_query.reshape(global_count, head_here, HEAD_DIM)
    cotangent_head_rows = global_cot.reshape(global_count, head_here, HEAD_DIM)
    key_per_head = key_rows.reshape(local_count, head_here, HEAD_DIM)
    value_per_head = value_rows.reshape(local_count, head_here, HEAD_DIM)
    logit_scores = (
        jnp.einsum("crj,prj->rcp", query_per_head, key_per_head, preferred_element_type=jnp.float32)
        * softmax_scale_factor
    )
    local_max = jnp.max(logit_scores, axis=2)
    local_sum = jnp.sum(jnp.exp(logit_scores - local_max[:, :, None]), axis=2)
    maxima, totals = joined((local_max, local_sum), "seq", merge_stats)
    chances = jnp.exp(logit_scores - maxima[:, :, None]) / totals[:, :, None]
    attention_weight_rows = chances.astype(jnp.bfloat16)
    partial_out = jnp.einsum(
        "bxl,lby->xby", attention_weight_rows, value_per_head, preferred_element_type=jnp.float32
    ).reshape(global_count, columns)
    global_out = lax.psum(partial_out, "seq").astype(jnp.bfloat16)
    deltas = jnp.transpose(
        jnp.sum(
            cotangent_head_rows.astype(jnp.float32)
            * global_out.reshape(global_count, head_here, HEAD_DIM).astype(jnp.float32),
            axis=2,
        )
    )[:, :, None]
    probability_gradient = jnp.einsum(
        "crj,prj->rcp", cotangent_head_rows, value_per_head, preferred_element_type=jnp.float32
    )
    scaled_scores = (chances * (probability_gradient - deltas) * softmax_scale_factor).astype(
        jnp.bfloat16
    )
    global_dq = jnp.einsum(
        "bxl,lby->xby", scaled_scores, key_per_head, preferred_element_type=jnp.float32
    ).reshape(global_count, columns)
    local_dk = jnp.einsum(
        "cgi,gcx->icx", scaled_scores, query_per_head, preferred_element_type=jnp.float32
    ).reshape(local_count, columns)
    local_dv = jnp.einsum(
        "cgi,gcx->icx",
        attention_weight_rows,
        cotangent_head_rows,
        preferred_element_type=jnp.float32,
    ).reshape(local_count, columns)
    global_grads = jnp.concatenate([grad_shared[rounds_count * BLK :], global_dq], axis=1)
    summed = lax.psum(global_grads, "seq")
    owned_rows = lax.dynamic_slice_in_dim(summed, shard_index * global_here, global_here, 0)
    returned = return_grads(
        grad_shared[: rounds_count * BLK].reshape(rounds_count, BLK, 2 * columns),
        partner_mask,
        levels,
    )
    from_next = passed_along(grad_ext[:BLK].astype(jnp.bfloat16), "seq", -1).astype(jnp.float32)
    from_prev = passed_along(grad_ext[BLK + local_count :].astype(jnp.bfloat16), "seq", 1).astype(
        jnp.float32
    )
    own_grads = grad_ext[BLK : BLK + local_count]
    own_grads = own_grads.at[:BLK].add(from_prev).at[local_count - BLK :].add(from_next)
    landing = chosen[0] * BLK
    own_grads = lax.dynamic_update_slice_in_dim(
        own_grads, lax.dynamic_slice_in_dim(own_grads, landing, BLK, 0) + returned[0], landing, 0
    )
    own_grads = own_grads + jnp.concatenate([local_dk, local_dv], axis=1)
    own_grads = own_grads.at[local_pos].add(owned_rows[:, : 2 * columns])
    grad_query_rows = sparse_dq.at[local_pos].add(owned_rows[:, 2 * columns :])
    own_out = lax.dynamic_slice_in_dim(global_out, shard_index * global_here, global_here, 0)
    attention = sparse_out.at[local_pos].set(own_out)
    return (
        attention,
        grad_query_rows.astype(jnp.bfloat16),
        own_grads[:, :columns].astype(jnp.bfloat16),
        own_grads[:, columns:].astype(jnp.bfloat16),
    )


def solution(mesh):
    placed = (P("seq", "tp"), P("seq", "tp"), P("seq", "tp"), P("seq", "tp"), P("seq"), P(), P())
    return jax.shard_map(
        per_device,
        mesh=mesh,
        in_specs=placed,
        out_specs=(P("seq", "tp"), P("seq", "tp"), P("seq", "tp"), P("seq", "tp")),
        check_vma=False,
    )
```

profile of v0, /device:TPU:8, one launch (start us, length us, event | category | flops | bytes accessed | tf_op | source)
XLA Modules:
  0.0 2457.4 jit_solution(18070954303673704445)
XLA Ops:
  20.9 4.1 collective-permute-start.1
  26.8 185.5 %all-gather.8 = bf16[64,4,1024]{2,1,0:T(4,128)(2,1)S(1)} all-gather(bf16[1,4,1024]{2,1,0:T(4,128)(2,1)S(1)} %bitcast.219), channel_id=4, replica_groups=mesh['seq'=64,'tp'=4] {'seq'}, dimensions={0}, use_global_device_ids=true | all-gather | bytes 532480 | tf_op jit(solution)/shard_map/all_gather | solution.py:116
  213.7 183.7 %all-gather.4 = f32[512,256]{1,0:T(8,128)S(1)} all-gather(f32[8,256]{1,0:T(8,128)S(1)} %exponential_reduce_fusion), channel_id=6, replica_groups=mesh['seq'=64,'tp'=4] {'seq'}, dimensions={0}, use_global_device_ids=true | all-gather | bytes 532480 | tf_op jit(solution)/shard_map/all_gather | solution.py:28
  398.2 177.0 %all-gather.3 = f32[512,256]{1,0:T(8,128)S(1)} all-gather(f32[8,256]{1,0:T(8,128)S(1)} %get-tuple-element.345), channel_id=5, replica_groups=mesh['seq'=64,'tp'=4] {'seq'}, dimensions={0}, use_global_device_ids=true | all-gather | bytes 532480 | tf_op jit(solution)/shard_map/all_gather | solution.py:28
  576.0 47.3 %while.40 = (s32[]{:T(128)}, f32[8,256]{1,0:T(8,128)S(1)}, f32[8,256]{1,0:T(8,128)S(1)}, f32[63,8,256]{2,1,0:T(8,128)}, f32[63,8,256]{2,1,0:T(8,128)}, /*index=5*/s32[]{:T(128)}) while((s32[]{:T(128)}, f32[8,256]{1,0:T(8,128)S(1)}, f32[8,256]{1,0:T(8,128)S(1)}, f32[63,8,256]{2,1,0:T(8,128)}, f32[63,8,256]{2,1,0:T(8,128)}, ...), condition=%wide.region_9.10_spmd, body=%wide.region_8.9_spmd.sunk | while | flops 12290 | bytes 49225 | solution.py:31
  626.9 356.7 %all-reduce.6 = bf16[256,1024]{0,1:T(8,128)(2,1)S(1)} all-reduce(f32[256,1024]{0,1:T(8,128)} %bitcast.212), channel_id=1, replica_groups=mesh['seq'=64,'tp'=4] {'seq'}, use_global_device_ids=true, to_apply=%region_10.11 | all-reduce | flops 262144 | bytes 1572864 | tf_op jit(solution)/shard_map/psum | solution.py:209
  987.4 192.3 %all-gather.9 = bf16[64,4,1024]{2,1,0:T(4,128)(2,1)} all-gather(bf16[1,4,1024]{2,1,0:T(4,128)(2,1)S(1)} %bitcast.218), channel_id=7, replica_groups=mesh['seq'=64,'tp'=4] {'seq'}, dimensions={0}, use_global_device_ids=true | all-gather | bytes 532480 | tf_op jit(solution)/shard_map/all_gather | solution.py:119
  1186.7 190.3 %all-gather.6 = bf16[64,4,1024]{2,1,0:T(4,128)(2,1)} all-gather(bf16[1,4,1024]{2,1,0:T(4,128)(2,1)S(1)} %bitcast.217), channel_id=2, replica_groups=mesh['seq'=64,'tp'=4] {'seq'}, dimensions={0}, use_global_device_ids=true | all-gather | bytes 532480 | tf_op jit(solution)/shard_map/all_gather | solution.py:118
  1376.9 188.0 %all-gather.7 = bf16[64,4,1024]{2,1,0:T(4,128)(2,1)} all-gather(bf16[1,4,1024]{2,1,0:T(4,128)(2,1)S(1)} %bitcast.216), channel_id=3, replica_groups=mesh['seq'=64,'tp'=4] {'seq'}, dimensions={0}, use_global_device_ids=true | all-gather | bytes 532480 | tf_op jit(solution)/shard_map/all_gather | solution.py:117
  1568.2 19.4 collective-permute-done.5
  1600.5 4.2 collective-permute-done.6
  1605.8 3.1 collective-permute-start.7
  1612.6 4.0 collective-permute-done.7
  1618.4 79.3 %while.39 = (s32[]{:T(128)}, bf16[2,128,1024]{2,1,0:T(8,128)(2,1)}, f32[2,128,1024]{2,1,0:T(8,128)}, f32[2,384,1024]{2,1,0:T(8,128)}, f32[2,384,1024]{2,1,0:T(8,...) while((s32[]{:T(128)}, bf16[2,128,1024]{2,1,0:T(8,128)(2,1)}, ...), condition=%wide.region_5.6_spmd, body=%wide.region_1.5_spmd.sunk | while | flops 1226704896 | bytes 130574560 | solution.py:179
  1646.2 3.0 copy.203
  1685.9 3.0 copy.203
  1724.7 8.3 collective-permute-done.11
  1739.2 5.5 collective-permute-done.12
  1746.5 3.0 fusion.15
  1749.9 11.7 collective-permute-done.13
  1770.1 4.7 collective-permute-start.9
  1777.3 3.7 collective-permute-done.14
  1787.6 5.5 collective-permute-done.15
  1797.8 647.4 %all-reduce.5.cloned.1.call-done = f32[256,3072]{1,0:T(8,128)} async-done(((f32[256,3072]{1,0:T(8,128)}), f32[256,3072]{1,0:T(8,128)}) %all-reduce.5.cloned.1.call-update) | async-done | bytes 3145744 | tf_op jit(solution)/shard_map/psum | solution.py:236
  (345 shorter events, 231.8 us)
Async XLA Ops:
  7.2 2438.1 %all-reduce.5.cloned.1.call-start = ((), (), s32[]{:S(2)}) async-start(), calls=%async_computation | async-start | bytes 6291456 | tf_op jit(solution)/shard_map/psum | solution.py:236
  11.7 1598.1 %copy-start.16 = (bf16[256,1024]{0,1:T(8,128)(2,1)}, bf16[256,1024]{0,1:T(8,128)(2,1)S(1)}, u32[]{:S(2)}) copy-start(bf16[256,1024]{0,1:T(8,128)(2,1)S(1)} %copy.125) | copy-start | bytes 1572868
  13.1 199.2 %copy-start.23 = (bf16[256,1024]{0,1:T(8,128)(2,1)}, bf16[256,1024]{0,1:T(8,128)(2,1)S(1)}, u32[]{:S(2)}) copy-start(bf16[256,1024]{0,1:T(8,128)(2,1)S(1)} %copy.126) | copy-start | bytes 1572868
  16.1 608.9 %collective-permute-start.2 = (bf16[1,128,2048]{2,1,0:T(8,128)(2,1)}, bf16[1,128,2048]{2,1,0:T(8,128)(2,1)}, u32[]{:S(2)}, u32[]{:S(2)}) collective-permute-start(bf16[1,128,2048]{2,1,0:T(8,128)(2,1)} %bitcast.27), channel_id=1, source_target_pairs={{0,4},{4,0},{8,12},{12,8},{16,20},{20,16},{24,28},{28,24},{32,36},... | collective-permute-start | bytes 1572872 | tf_op jit(solution)/shard_map/ppermute | solution.py:11
  18.4 1591.4 %collective-permute-start = (bf16[128,2048]{0,1:T(8,128)(2,1)}, bf16[128,2048]{0,1:T(8,128)(2,1)}, u32[]{:S(2)}, u32[]{:S(2)}) collective-permute-start(bf16[128,2048]{0,1:T(8,128)(2,1)} %get-tuple-element.341), channel_id=1, source_target_pairs={{0,4},{4,8},{8,12},{12,16},{16,20},{20,24},{24,28},{28,32},{32,36}... | collective-permute-start | bytes 1572872 | tf_op jit(solution)/shard_map/ppermute | solution.py:21
  20.9 1588.9 %collective-permute-start.1 = (bf16[128,2048]{0,1:T(8,128)(2,1)}, bf16[128,2048]{0,1:T(8,128)(2,1)}, u32[]{:S(2)}, u32[]{:S(2)}) collective-permute-start(bf16[128,2048]{0,1:T(8,128)(2,1)} %get-tuple-element.342), channel_id=1, source_target_pairs={{4,0},{8,4},{12,8},{16,12},{20,16},{24,20},{28,24},{32,28},{36,32}... | collective-permute-start | bytes 1572872 | tf_op jit(solution)/shard_map/ppermute | solution.py:22
  397.4 226.0 %copy-start.37 = (bf16[256,1024]{1,0:T(8,128)(2,1)S(1)}, bf16[256,1024]{1,0:T(8,128)(2,1)}, u32[]{:S(2)}) copy-start(bf16[256,1024]{1,0:T(8,128)(2,1)} %param.25) | copy-start | bytes 1572868
  626.9 358.6 %collective-permute-start.3 = (bf16[1,128,2048]{2,1,0:T(8,128)(2,1)}, bf16[1,128,2048]{2,1,0:T(8,128)(2,1)}, u32[]{:S(2)}, u32[]{:S(2)}) collective-permute-start(bf16[1,128,2048]{2,1,0:T(8,128)(2,1)} %broadcast_select_fusion.1), channel_id=1, source_target_pairs={{0,8},{4,12},{8,0},{12,4},{16,24},{20,28},{24,16},{28,20},{32,40},... | collective-permute-start | bytes 1572872 | tf_op jit(solution)/shard_map/ppermute | solution.py:11
  983.5 199.5 %copy-start.30 = (bf16[256,1024]{0,1:T(8,128)(2,1)}, bf16[256,1024]{0,1:T(8,128)(2,1)S(1)}, u32[]{:S(2)}) copy-start(bf16[256,1024]{0,1:T(8,128)(2,1)S(1)} %all-reduce.6) | copy-start | bytes 1572868
  987.3 577.6 %collective-permute-start.4 = (bf16[1,128,2048]{2,1,0:T(8,128)(2,1)}, bf16[1,128,2048]{2,1,0:T(8,128)(2,1)}, u32[]{:S(2)}, u32[]{:S(2)}) collective-permute-start(bf16[1,128,2048]{2,1,0:T(8,128)(2,1)} %broadcast_select_fusion.2), channel_id=1, source_target_pairs={{0,16},{4,20},{8,24},{12,28},{16,0},{20,4},{24,8},{28,12},{32,48},... | collective-permute-start | bytes 1572872 | tf_op jit(solution)/shard_map/ppermute | solution.py:11
  1186.7 379.5 %copy-start.26 = (f32[256,8,128]{2,1,0:T(8,128)S(1)}, f32[256,8,128]{2,1,0:T(8,128)}, u32[]{:S(2)}) copy-start(f32[256,8,128]{2,1,0:T(8,128)} %copy.145) | copy-start | bytes 3145732
  1186.7 379.9 %copy-start.38 = (bf16[256,8,128]{0,2,1:T(8,128)(2,1)S(1)}, bf16[256,8,128]{0,2,1:T(8,128)(2,1)}, u32[]{:S(2)}) copy-start(bf16[256,8,128]{0,2,1:T(8,128)(2,1)} %copy.157) | copy-start | bytes 1572868
  1566.1 21.4 collective-permute-start.5
  1588.4 16.3 collective-permute-start.6
  1605.8 10.8 collective-permute-start.7
  1706.4 14.6 collective-permute-start.10
  1722.2 10.8 collective-permute-start.11
  1735.2 9.5 collective-permute-start.12
  1746.4 15.2 collective-permute-start.13
  1749.5 19.0 copy-start.6
  1762.6 18.4 collective-permute-start.14
  1766.4 16.5 collective-permute-start.8
  1770.1 15.0 collective-permute-start.9
  1782.4 10.8 collective-permute-start.15
  (50 other events, 226.9 us)
Sparse Core Ops, SparseCore 0:
  1739.3 705.8 all-reduce.4
where the time goes:
time: 2470 us; the launch traced here: 2460 us
  blocking collectives  1470 us (60%)
  waiting for transfers between devices  710 us (29%)
  other arithmetic  102 us (4%)
  local copies, waits for them, and re-layouts  100 us (4%)
  matrix products  26.1 us (1%)
  starting transfers between devices  25.1 us (1%)
    psum x1, waiting for transfers between devices, per_device(): summed = lax.psum(global_grads, 'seq')  647 us
    all_gather x2, blocking collectives, joined(): pieces = jax.tree.map(lambda part: lax.all_gather(part, axis), value)  361 us
    psum x1, blocking collectives, per_device(): global_out = lax.psum(partial_out, 'seq').astype(jnp.bfloat16)  357 us
    all_gather x1, blocking collectives, per_device(): lax.all_gather(cotangent[local_pos], 'seq', axis=0, tiled=True)  192 us
    all_gather x1, blocking collectives, per_device(): lax.all_gather(value_rows[local_pos], 'seq', axis=0, tiled=True)  190 us
    all_gather x1, blocking collectives, per_device(): lax.all_gather(key_rows[local_pos], 'seq', axis=0, tiled=True)  188 us
    all_gather x1, blocking collectives, per_device(): lax.all_gather(query_rows[local_pos], 'seq', axis=0, tiled=True)  186 us
    ppermute x12, waiting for transfers between devices, from_partner(): lax.ppermute(shard, axis, [(i, i ^ 1 << bit) for i in range(lax.axis_size...  62.3 us
  transfers between devices with their start and end apart: 17, of which 9 were waited for; matrix products, arithmetic and copies ran while one was open for 5% of the time, Pallas kernels for 0%

commit v1 on v0

--- a/solution.py
+++ b/solution.py
@@ -115,7 +115,10 @@
     global_query, global_key, global_value, global_cot = (
         lax.all_gather(query_rows[local_pos], "seq", axis=0, tiled=True),
         lax.all_gather(key_rows[local_pos], "seq", axis=0, tiled=True),
-        lax.all_gather(value_rows[local_pos], "seq", axis=0, tiled=True),
+        jnp.concatenate(
+            lax.all_to_all(jnp.stack([value_rows[local_pos]] * lax.axis_size("seq")), "seq", 0, 0),
+            axis=0,
+        ),
         lax.all_gather(cotangent[local_pos], "seq", axis=0, tiled=True),
     )
     global_count = global_query.shape[0]

time: 2470 us -> 2320 us (0.939)
  blocking collectives: 1470 us -> 1300 us
  starting transfers between devices: 25.1 us -> 59.6 us
    all_gather x1 -> x0, blocking collectives: 190 us -> none  [per_device(): lax.all_gather(value_rows[local_pos], 'seq', axis=0, tiled=True)]
  transfers between devices with their start and end apart: 17 -> 18, of which waited for: 9 -> 9; matrix products, arithmetic and copies ran while one was open for 5% -> 5% of each run, Pallas kernels for 0% -> 0%
where the time goes in v1:
time: 2320 us; the launch traced here: 2310 us
  blocking collectives  1300 us (56%)
  waiting for transfers between devices  704 us (30%)
  other arithmetic  101 us (4%)
  local copies, waits for them, and re-layouts  99.2 us (4%)
  starting transfers between devices  59.6 us (3%)
  matrix products  27.2 us (1%)
    psum x1, waiting for transfers between devices, per_device(): summed = lax.psum(global_grads, 'seq')  651 us
    all_gather x2, blocking collectives, joined(): pieces = jax.tree.map(lambda part: lax.all_gather(part, axis), value)  376 us
    psum x1, blocking collectives, per_device(): global_out = lax.psum(partial_out, 'seq').astype(jnp.bfloat16)  357 us
    all_gather x1, blocking collectives, per_device(): lax.all_gather(cotangent[local_pos], 'seq', axis=0, tiled=True)  193 us
    all_gather x1, blocking collectives, per_device(): lax.all_gather(key_rows[local_pos], 'seq', axis=0, tiled=True)  190 us
    all_gather x1, blocking collectives, per_device(): lax.all_gather(query_rows[local_pos], 'seq', axis=0, tiled=True)  182 us
    ppermute x12, waiting for transfers between devices, from_partner(): lax.ppermute(shard, axis, [(i, i ^ 1 << bit) for i in range(lax.axis_size...  53.1 us
  transfers between devices with their start and end apart: 18, of which 9 were waited for; matrix products, arithmetic and copies ran while one was open for 5% of the time, Pallas kernels for 0%

profile of v1, /device:TPU:8, one launch (start us, length us, event | category | flops | bytes accessed | tf_op | source)
XLA Modules:
  0.0 2310.3 jit_solution(17577260072753585162)
XLA Ops:
  20.8 4.2 collective-permute-start.1
  28.2 14.1 all-to-all-start
  44.0 182.0 %all-gather.6 = bf16[64,4,1024]{2,1,0:T(4,128)(2,1)S(1)} all-gather(bf16[1,4,1024]{2,1,0:T(4,128)(2,1)S(1)} %bitcast.217), channel_id=3, replica_groups=mesh['seq'=64,'tp'=4] {'seq'}, dimensions={0}, use_global_device_ids=true | all-gather | bytes 532480 | tf_op jit(solution)/shard_map/all_gather | solution.py:116
  227.1 189.6 %all-gather.2 = f32[512,256]{1,0:T(8,128)} all-gather(f32[8,256]{1,0:T(8,128)S(1)} %get-tuple-element.345), channel_id=4, replica_groups=mesh['seq'=64,'tp'=4] {'seq'}, dimensions={0}, use_global_device_ids=true | all-gather | bytes 532480 | tf_op jit(solution)/shard_map/all_gather | solution.py:28
  417.0 186.6 %all-gather.3 = f32[512,256]{1,0:T(8,128)} all-gather(f32[8,256]{1,0:T(8,128)S(1)} %exponential_reduce_fusion), channel_id=5, replica_groups=mesh['seq'=64,'tp'=4] {'seq'}, dimensions={0}, use_global_device_ids=true | all-gather | bytes 532480 | tf_op jit(solution)/shard_map/all_gather | solution.py:28
  608.6 47.1 %while.40 = (s32[]{:T(128)}, f32[8,256]{1,0:T(8,128)S(1)}, f32[8,256]{1,0:T(8,128)S(1)}, f32[63,8,256]{2,1,0:T(8,128)}, f32[63,8,256]{2,1,0:T(8,128)}, /*index=5*/s32[]{:T(128)}) while((s32[]{:T(128)}, f32[8,256]{1,0:T(8,128)S(1)}, f32[8,256]{1,0:T(8,128)S(1)}, f32[63,8,256]{2,1,0:T(8,128)}, f32[63,8,256]{2,1,0:T(8,128)}, ...), condition=%wide.region_9.10_spmd, body=%wide.region_8.9_spmd.sunk | while | flops 12290 | bytes 49225 | solution.py:31
  659.2 356.8 %all-reduce.6 = bf16[256,1024]{0,1:T(8,128)(2,1)S(1)} all-reduce(f32[256,1024]{0,1:T(8,128)} %bitcast.211), channel_id=1, replica_groups=mesh['seq'=64,'tp'=4] {'seq'}, use_global_device_ids=true, to_apply=%region_10.11 | all-reduce | flops 262144 | bytes 1572864 | tf_op jit(solution)/shard_map/psum | solution.py:212
  1020.8 192.7 %all-gather.7 = bf16[64,4,1024]{2,1,0:T(4,128)(2,1)} all-gather(bf16[1,4,1024]{2,1,0:T(4,128)(2,1)S(1)} %bitcast.216), channel_id=6, replica_groups=mesh['seq'=64,'tp'=4] {'seq'}, dimensions={0}, use_global_device_ids=true | all-gather | bytes 532480 | tf_op jit(solution)/shard_map/all_gather | solution.py:122
  1214.7 190.3 %all-gather.5 = bf16[64,4,1024]{2,1,0:T(4,128)(2,1)} all-gather(bf16[1,4,1024]{2,1,0:T(4,128)(2,1)S(1)} %bitcast.215), channel_id=2, replica_groups=mesh['seq'=64,'tp'=4] {'seq'}, dimensions={0}, use_global_device_ids=true | all-gather | bytes 532480 | tf_op jit(solution)/shard_map/all_gather | solution.py:117
  1411.5 12.9 collective-permute-done.5
  1426.3 6.3 collective-permute-start.6
  1436.7 9.5 collective-permute-done.6
  1447.3 13.6 collective-permute-start.7
  1469.9 79.0 %while.39 = (s32[]{:T(128)}, bf16[2,128,1024]{2,1,0:T(8,128)(2,1)}, f32[2,128,1024]{2,1,0:T(8,128)}, f32[2,384,1024]{2,1,0:T(8,128)}, f32[2,384,1024]{2,1,0:T(8,...) while((s32[]{:T(128)}, bf16[2,128,1024]{2,1,0:T(8,128)(2,1)}, ...), condition=%wide.region_5.6_spmd, body=%wide.region_1.5_spmd.sunk | while | flops 1226704896 | bytes 130574560 | solution.py:182
  1497.6 3.1 copy.203
  1537.1 3.1 copy.203
  1573.6 8.3 collective-permute-done.11
  1588.1 5.5 collective-permute-done.12
  1595.4 3.0 fusion.15
  1598.7 11.7 collective-permute-done.13
  1611.5 5.4 collective-permute-start.14
  1621.5 5.5 collective-permute-start.9
  1632.0 3.4 collective-permute-start.15
  1647.3 650.7 %all-reduce.5.cloned.1.call-done = f32[256,3072]{1,0:T(8,128)} async-done(((f32[256,3072]{1,0:T(8,128)}), f32[256,3072]{1,0:T(8,128)}) %all-reduce.5.cloned.1.call-update) | async-done | bytes 3145744 | tf_op jit(solution)/shard_map/psum | solution.py:239
  (345 shorter events, 231.2 us)
Async XLA Ops:
  11.6 1450.1 %copy-start.16 = (bf16[256,1024]{0,1:T(8,128)(2,1)}, bf16[256,1024]{0,1:T(8,128)(2,1)S(1)}, u32[]{:S(2)}) copy-start(bf16[256,1024]{0,1:T(8,128)(2,1)S(1)} %copy.125) | copy-start | bytes 1572868
  16.1 591.3 %collective-permute-start.2 = (bf16[1,128,2048]{2,1,0:T(8,128)(2,1)}, bf16[1,128,2048]{2,1,0:T(8,128)(2,1)}, u32[]{:S(2)}, u32[]{:S(2)}) collective-permute-start(bf16[1,128,2048]{2,1,0:T(8,128)(2,1)} %bitcast.27), channel_id=1, source_target_pairs={{0,4},{4,0},{8,12},{12,8},{16,20},{20,16},{24,28},{28,24},{32,36},... | collective-permute-start | bytes 1572872 | tf_op jit(solution)/shard_map/ppermute | solution.py:11
  18.4 1443.4 %collective-permute-start = (bf16[128,2048]{0,1:T(8,128)(2,1)}, bf16[128,2048]{0,1:T(8,128)(2,1)}, u32[]{:S(2)}, u32[]{:S(2)}) collective-permute-start(bf16[128,2048]{0,1:T(8,128)(2,1)} %get-tuple-element.341), channel_id=1, source_target_pairs={{0,4},{4,8},{8,12},{12,16},{16,20},{20,24},{24,28},{28,32},{32,36}... | collective-permute-start | bytes 1572872 | tf_op jit(solution)/shard_map/ppermute | solution.py:21
  20.8 1440.9 %collective-permute-start.1 = (bf16[128,2048]{0,1:T(8,128)(2,1)}, bf16[128,2048]{0,1:T(8,128)(2,1)}, u32[]{:S(2)}, u32[]{:S(2)}) collective-permute-start(bf16[128,2048]{0,1:T(8,128)(2,1)} %get-tuple-element.342), channel_id=1, source_target_pairs={{4,0},{8,4},{12,8},{16,12},{20,16},{24,20},{28,24},{32,28},{36,32}... | collective-permute-start | bytes 1572872 | tf_op jit(solution)/shard_map/ppermute | solution.py:22
  28.2 1436.3 %all-to-all-start = ((bf16[64,4,1024]{2,1,0:T(4,128)(2,1)}), bf16[64,4,1024]{2,1,0:T(4,128)(2,1)}, u32[]{:S(2)}, u32[]{:S(2)}) async-start(bf16[64,4,1024]{2,1,0:T(4,128)(2,1)} %stack.5), calls=%async_computation | async-start | bytes 1048576 | tf_op jit(solution)/shard_map/all_to_all | solution.py:119
  42.3 2255.8 %all-reduce.5.cloned.1.call-start = ((), (), s32[]{:S(2)}) async-start(), calls=%async_computation.1 | async-start | bytes 6291456 | tf_op jit(solution)/shard_map/psum | solution.py:239
  226.5 190.5 %copy-start.21 = (bf16[256,8,128]{0,2,1:T(8,128)(2,1)}, bf16[256,8,128]{0,2,1:T(8,128)(2,1)S(1)}, u32[]{:S(2)}) copy-start(bf16[256,8,128]{0,2,1:T(8,128)(2,1)S(1)} %copy.155) | copy-start | bytes 1572868
  417.0 191.5 %slice-start = ((f32[512,256]{1,0:T(8,128)}), f32[8,256]{1,0:T(8,128)S(1)}, s32[]{:S(2)}) async-start(f32[512,256]{1,0:T(8,128)} %all-gather.2), calls=%async_computation.2 | async-start | bytes 16384 | tf_op jit(solution)/shard_map/slice | solution.py:29
  608.4 49.9 %collective-permute-start.3 = (bf16[1,128,2048]{2,1,0:T(8,128)(2,1)S(1)}, bf16[1,128,2048]{2,1,0:T(8,128)(2,1)}, u32[]{:S(2)}, u32[]{:S(2)}) collective-permute-start(bf16[1,128,2048]{2,1,0:T(8,128)(2,1)S(1)} %broadcast_select_fusion.1), channel_id=1, source_target_pairs={{0,8},{4,12},{8,0},{12,4},{16,24},{20,28},{24,16},{28,20},{32,40},... | collective-permute-start | bytes 1572872 | tf_op jit(solution)/shard_map/ppermute | solution.py:11
  659.2 745.8 %collective-permute-start.4 = (bf16[1,128,2048]{2,1,0:T(8,128)(2,1)}, bf16[1,128,2048]{2,1,0:T(8,128)(2,1)}, u32[]{:S(2)}, u32[]{:S(2)}) collective-permute-start(bf16[1,128,2048]{2,1,0:T(8,128)(2,1)} %broadcast_select_fusion.2), channel_id=1, source_target_pairs={{0,16},{4,20},{8,24},{12,28},{16,0},{20,4},{24,8},{28,12},{32,48},... | collective-permute-start | bytes 1572872 | tf_op jit(solution)/shard_map/ppermute | solution.py:11
  1214.7 192.2 %copy-start.26 = (f32[256,8,128]{2,1,0:T(8,128)S(1)}, f32[256,8,128]{2,1,0:T(8,128)}, u32[]{:S(2)}) copy-start(f32[256,8,128]{2,1,0:T(8,128)} %copy.145) | copy-start | bytes 3145732
  1406.9 17.4 collective-permute-start.5
  1408.5 24.0 %copy-start.36 = (bf16[256,8,128]{0,2,1:T(8,128)(2,1)S(1)}, bf16[256,8,128]{0,2,1:T(8,128)(2,1)}, u32[]{:S(2)}) copy-start(bf16[256,8,128]{0,2,1:T(8,128)(2,1)} %copy.157) | copy-start | bytes 1572868
  1426.3 19.9 collective-permute-start.6
  1435.7 26.0 %copy-start.24 = (bf16[256,1024]{0,1:T(8,128)(2,1)S(1)}, bf16[256,1024]{0,1:T(8,128)(2,1)}, u32[]{:S(2)}) copy-start(bf16[256,1024]{0,1:T(8,128)(2,1)} %copy-done.23) | copy-start | bytes 1572868
  1447.3 20.7 collective-permute-start.7
  1557.6 12.3 collective-permute-start.10
  1571.1 10.8 collective-permute-start.11
  1584.1 9.5 collective-permute-start.12
  1595.3 15.2 collective-permute-start.13
  1611.5 19.1 collective-permute-start.14
  1617.9 17.4 collective-permute-start.8
  1621.5 15.9 collective-permute-start.9
  1632.0 10.8 collective-permute-start.15
  (51 other events, 241.3 us)
Sparse Core Ops, SparseCore 0:
  1588.2 709.8 all-reduce.4
